TPU v7x, 32 devices: a whole 2x2x4 slice. The times are simulated.
32 devices in a mesh: mp: 4 (over x, core), seq: 8 (over z, y).
Axes of the slice: x: 2, y: 2, z: 4, core: 2. Of those that a mesh axis runs over, the one named last changes fastest.
Arguments:
- hidden_in: bfloat16 [2048, 5376], P('seq', 'mp'), may hold values from -28 to 28
- gain_in: float32 [5376], replicated, may hold values from 0.3 to 3
- w_query: bfloat16 [5376, 4096], P('seq', 'mp'), may hold values from -0.078125 to 0.078125
- key_weight: bfloat16 [5376, 2048], P('seq', 'mp'), may hold values from -0.078125 to 0.078125
- value_weight: bfloat16 [5376, 2048], P('seq', 'mp'), may hold values from -0.078125 to 0.078125
- gain_query: float32 [128], replicated, may hold values from 0.3 to 3
- gain_key: float32 [128], replicated, may hold values from 0.3 to 3
- start_pos: int32 [1], replicated, may hold values from 1024 to 4095
- cached_key_rows: bfloat16 [1024, 2048], P(None, 'mp'), may hold values from -140 to 140
- cached_value_rows: bfloat16 [1024, 2048], P(None, 'mp'), may hold values from -5 to 5
- w_out: bfloat16 [4096, 5376], P('seq', 'mp'), may hold values from -1.5 to 1.5
- gain_post: float32 [5376], P('mp'), may hold values from 0.3 to 3
Outputs:
- hidden_out: bfloat16 [2048, 5376], P('seq', 'mp')
All inputs are finite; a program needn't handle non-finite values.
Results may differ from a plain program's by a relative error of at most 0.012.
The roundings to bfloat16 on the way count: a program that leaves them out, or rounds other values in their place, can miss the bound.
Values may be sent and summed in bfloat16 or wider, within the bound.
A program may use at most 128 MiB of HBM per device.

v0:
```python
import jax
import jax.numpy as jnp
from jax import lax
from jax.sharding import PartitionSpec as P

MODEL_WIDTH = 5376
WINDOW_LENGTH = 1024


epsilon = 1e-06
query_scale = 168.0 ** (-0.5)
rope_base = 10000.0


def shifted(x, axis, by):
    peers = lax.axis_size(axis)
    pairs = [(i, i + by) for i in range(peers) if 0 <= i + by < peers]
    return lax.ppermute(x, axis, pairs)


def norm_rows(values, gain):
    return values * lax.rsqrt(jnp.mean(values * values, axis=-1, keepdims=True) + epsilon) * gain


def rotate(tensor, positions):
    half_dim = tensor.shape[-1] // 2
    inverse_freq = rope_base ** (
        -(jnp.arange(half_dim, dtype=jnp.float32) * 2.0) / tensor.shape[-1]
    )
    angles = positions.astype(jnp.float32)[:, None, None] * inverse_freq[None, None, :]
    cosine = jnp.cos(angles)
    sine = jnp.sin(angles)
    first = tensor[..., :half_dim]
    second = tensor[..., half_dim:]
    return jnp.concatenate(
        [first * cosine - second * sine, second * cosine + first * sine], axis=-1
    )


def on_device(
    hidden_in,
    gain_in,
    w_query,
    key_weight,
    value_weight,
    gain_query,
    gain_key,
    start_pos,
    cached_key_rows,
    cached_value_rows,
    w_out,
    gain_post,
):
    n_rows = hidden_in.shape[0]
    head_dim = gain_query.shape[0]
    kv_cols = key_weight.shape[1]
    kv_heads = kv_cols // head_dim
    q_heads = w_query.shape[1] // head_dim
    query_group_count = q_heads // kv_heads
    full_rows = lax.all_gather(hidden_in, "mp", axis=1, tiled=True)
    normed_hidden = norm_rows(full_rows.astype(jnp.float32), gain_in).astype(jnp.bfloat16)

    def add_rows(block_rows):
        return jnp.dot(normed_hidden, block_rows, preferred_element_type=jnp.float32)

    keys_raw = add_rows(lax.all_gather(key_weight, "seq", axis=0, tiled=True))
    values_raw = add_rows(lax.all_gather(value_weight, "seq", axis=0, tiled=True))
    query_matrix = add_rows(lax.all_gather(w_query, "seq", axis=0, tiled=True))
    seq_index = lax.axis_index("seq")
    positions = start_pos[0] + seq_index * n_rows + jnp.arange(n_rows, dtype=jnp.int32)
    query_matrix = (
        rotate(norm_rows(query_matrix.reshape(n_rows, q_heads, head_dim), gain_query), positions)
        * query_scale
    ).astype(jnp.bfloat16)
    fresh_key = rotate(
        norm_rows(keys_raw.reshape(n_rows, kv_heads, head_dim), gain_key), positions
    ).astype(jnp.bfloat16)
    fresh = jnp.stack([fresh_key.reshape(n_rows, kv_cols), values_raw.astype(jnp.bfloat16)])
    reach_shards = (WINDOW_LENGTH + n_rows - 1) // n_rows
    reach_rows = reach_shards * n_rows
    pieces = []
    moving = fresh
    for hop_index in range(reach_shards):
        moving = shifted(moving, "seq", 1)
        pieces.insert(0, moving)
    prior = jnp.concatenate(pieces, axis=1)
    front_pad = reach_rows - WINDOW_LENGTH
    cached = jnp.stack([cached_key_rows, cached_value_rows])
    padded = jnp.concatenate(
        [
            jnp.zeros((2, front_pad, kv_cols), cached.dtype),
            cached,
            jnp.zeros((2, reach_rows, kv_cols), cached.dtype),
        ],
        axis=1,
    )
    cache_start = jnp.minimum(seq_index * n_rows, front_pad + WINDOW_LENGTH)
    from_cache = lax.dynamic_slice_in_dim(padded, cache_start, reach_rows, 1)
    prior_rows = jnp.arange(reach_rows, dtype=jnp.int32)
    use_cache = prior_rows < reach_rows - seq_index * n_rows
    prior = jnp.where(use_cache[None, :, None], from_cache, prior)
    window_kv = jnp.concatenate([prior, fresh], axis=1)
    span_rows = reach_rows + n_rows
    key_heads = window_kv[0].reshape(span_rows, kv_heads, head_dim)
    value_heads = window_kv[1].reshape(span_rows, kv_heads, head_dim)
    query_heads = query_matrix.reshape(n_rows, kv_heads, query_group_count, head_dim)
    scores = jnp.einsum(
        "tkgd,skd->kgts", query_heads, key_heads, preferred_element_type=jnp.float32
    )
    query_index = jnp.arange(n_rows, dtype=jnp.int32)[:, None]
    key_index = jnp.arange(span_rows, dtype=jnp.int32)[None, :]
    visible = (key_index > query_index + reach_rows - WINDOW_LENGTH) & (
        key_index <= query_index + reach_rows
    )
    scores = jnp.where(visible, scores, -jnp.inf)
    row_max = jnp.max(scores, axis=-1, keepdims=True)
    probs = jnp.exp(scores - row_max)
    totals = jnp.sum(probs, axis=-1)
    probs_b = probs.astype(jnp.bfloat16)
    summed = jnp.einsum("kgts,skd->tkgd", probs_b, value_heads, preferred_element_type=jnp.float32)
    summed = summed / jnp.transpose(totals, (2, 0, 1))[..., None]
    attn = summed.reshape(n_rows, q_heads * head_dim).astype(jnp.bfloat16)
    all_heads = lax.all_gather(attn, "mp", axis=1, tiled=True)
    projected = jnp.dot(
        all_heads,
        lax.all_gather(w_out, "seq", axis=0, tiled=True),
        preferred_element_type=jnp.float32,
    )
    squares = lax.psum(jnp.sum(projected * projected, axis=-1), "mp")
    scaling = lax.rsqrt(squares / MODEL_WIDTH + epsilon)
    return (hidden_in.astype(jnp.float32) + projected * scaling[:, None] * gain_post).astype(
        jnp.bfloat16
    )


def solution(mesh):
    in_specs = (
        P("seq", "mp"),
        P(),
        P("seq", "mp"),
        P("seq", "mp"),
        P("seq", "mp"),
        P(),
        P(),
        P(),
        P(None, "mp"),
        P(None, "mp"),
        P("seq", "mp"),
        P("mp"),
    )
    out_specs = P("seq", "mp")
    return jax.shard_map(
        on_device, mesh=mesh, in_specs=in_specs, out_specs=out_specs, check_vma=False
    )
```

profile of v0, /device:TPU:19, one launch (start us, length us, event | category | flops | bytes accessed | tf_op | source)
XLA Modules:
  0.0 615.8 jit_solution(16389566803389255011)
XLA Ops:
  6.5 0.7 all-gather.7.cloned.1.call-update
  7.3 0.7 all-gather.9.cloned.1.call-update
  8.1 0.7 all-gather.11.cloned.1.call-update
  8.8 0.5 all-gather.13.cloned.1.call-update
  9.4 0.5 all-gather.17.cloned.1.call-update
  10.6 0.5 multiply_cosine_fusion
  11.2 24.6 %all-gather.7.cloned.1.call-done = bf16[256,5376]{0,1:T(8,128)(2,1)} async-done(((bf16[256,1344]{0,1:T(8,128)(2,1)}), bf16[256,5376]{0,1:T(8,128)(2,1)}) %all-gather.7.cloned.1.call-update) | async-done | bytes 2752528 | tf_op jit(solution)/shard_map/all_gather | solution.py:60
  35.8 2.5 fusion.3
  38.3 88.3 %all-gather.9.cloned.1.call-done = bf16[5376,512]{1,0:T(8,128)(2,1)} async-done(((bf16[672,512]{1,0:T(8,128)(2,1)}), bf16[5376,512]{1,0:T(8,128)(2,1)}) %all-gather.9.cloned.1.call-update) | async-done | bytes 5505040 | tf_op jit(solution)/shard_map/all_gather | solution.py:66
  126.7 7.3 %fusion.32 = f32[256,512]{1,0:T(8,128)} fusion(bf16[5376,512]{1,0:T(8,128)(2,1)} %all-gather.9.cloned.1.call-done, bf16[256,5376]{0,1:T(8,128)(2,1)} %all-gather.7.cloned.1.call-done, f32[5376]{0:T(1024)S(1)} %copy-done.12, f32[256]{0:T(256)S(1)} %add_rsqrt_fusion.3), kind=kOutput, calls=%fused_computation.60 | convolution fusion | flops 1414791168 | bytes 8804352 | tf_op jit(solution)/shard_map/dot_general | solution.py:64
  134.0 1.4 reshape.136
  135.4 0.3 multiply_reduce_fusion.2
  135.8 0.3 multiply_multiply_fusion.1
  136.1 0.5 subtract_convert_fusion
  136.6 0.4 pad_maximum_fusion.1
  137.1 79.4 %all-gather.11.cloned.1.call-done = bf16[5376,512]{1,0:T(8,128)(2,1)} async-done(((bf16[672,512]{1,0:T(8,128)(2,1)}), bf16[5376,512]{1,0:T(8,128)(2,1)}) %all-gather.11.cloned.1.call-update) | async-done | bytes 5505040 | tf_op jit(solution)/shard_map/all_gather | solution.py:67
  216.6 5.7 fusion.21
  222.3 0.7 copy-done.7
  223.0 2.3 collective-permute-start
  225.3 28.1 %collective-permute-done = bf16[2,256,512]{2,1,0:T(8,128)(2,1)S(1)} collective-permute-done((bf16[2,256,512]{2,1,0:T(8,128)(2,1)S(1)}, bf16[2,256,512]{2,1,0:T(8,128)(2,1)S(1)}, u32[]{:S(2)}, u32[]{:S(2)}) %collective-permute-start) | collective-permute-done | bytes 524320 | tf_op jit(solution)/shard_map/ppermute | solution.py:18
  253.4 2.4 collective-permute-start.1
  255.8 31.6 %collective-permute-done.1 = bf16[2,256,512]{2,1,0:T(8,128)(2,1)S(1)} collective-permute-done((bf16[2,256,512]{2,1,0:T(8,128)(2,1)S(1)}, bf16[2,256,512]{2,1,0:T(8,128)(2,1)S(1)}, u32[]{:S(2)}, u32[]{:S(2)}) %collective-permute-start.1) | collective-permute-done | bytes 524320 | tf_op jit(solution)/shard_map/ppermute | solution.py:18
  287.4 7.1 %collective-permute-start.2 = (bf16[2,256,512]{2,1,0:T(8,128)(2,1)S(1)}, bf16[2,256,512]{2,1,0:T(8,128)(2,1)S(1)}, u32[]{:S(2)}, u32[]{:S(2)}) collective-permute-start(bf16[2,256,512]{2,1,0:T(8,128)(2,1)S(1)} %collective-permute-done.1), channel_id=1, source_target_pairs={{0,1},{1,2},{2,3},{3,4},{4,5},{5,6},{6,7},{8,9},{9,10},{10,11},{11... | collective-permute-start | bytes 1572872 | tf_op jit(solution)/shard_map/ppermute | solution.py:18
  294.6 9.2 %collective-permute-done.2 = bf16[2,256,512]{2,1,0:T(8,128)(2,1)S(1)} collective-permute-done((bf16[2,256,512]{2,1,0:T(8,128)(2,1)S(1)}, bf16[2,256,512]{2,1,0:T(8,128)(2,1)S(1)}, u32[]{:S(2)}, u32[]{:S(2)}) %collective-permute-start.2) | collective-permute-done | bytes 524320 | tf_op jit(solution)/shard_map/ppermute | solution.py:18
  303.7 5.2 collective-permute-start.3
  308.9 0.2 fusion.20
  309.2 14.9 %collective-permute-done.3 = bf16[2,256,512]{2,1,0:T(8,128)(2,1)S(1)} collective-permute-done((bf16[2,256,512]{2,1,0:T(8,128)(2,1)S(1)}, bf16[2,256,512]{2,1,0:T(8,128)(2,1)S(1)}, u32[]{:S(2)}, u32[]{:S(2)}) %collective-permute-start.3) | collective-permute-done | bytes 524320 | tf_op jit(solution)/shard_map/ppermute | solution.py:18
  324.1 4.6 fusion.14
  328.7 0.2 maximum_maximum_fusion
  328.9 1.3 fusion.34
  330.2 2.7 reshape_squeeze.7
  332.9 1.5 copy.37
  334.3 81.3 %all-gather.13.cloned.1.call-done = bf16[5376,1024]{1,0:T(8,128)(2,1)} async-done(((bf16[672,1024]{1,0:T(8,128)(2,1)}), bf16[5376,1024]{1,0:T(8,128)(2,1)}) %all-gather.13.cloned.1.call-update) | async-done | bytes 11010064 | tf_op jit(solution)/shard_map/all_gather | solution.py:68
  415.6 8.1 %convolution_bitcast_fusion = f32[32,8,8,128]{3,1,2,0:T(8,128)S(1)} fusion(bf16[5376,1024]{1,0:T(8,128)(2,1)} %all-gather.13.cloned.1.call-done, bf16[256,5376]{0,1:T(8,128)(2,1)} %all-gather.7.cloned.1.call-done, f32[5376]{0:T(1024)S(1)} %copy-done.13, f32[256]{0:T(256)S(1)} %add_rsqrt_fusion.3), kind=kOutput, calls=%fused_computation.27 | convolution fusion | flops 2824077312 | bytes 14833664 | tf_op jit(solution)/shard_map/dot_general | solution.py:64
  423.7 0.2 copy.40
  423.9 0.3 multiply_reduce_fusion.1
  424.5 0.3 multiply_multiply_fusion
  424.9 0.6 multiply_subtract_fusion
  425.4 0.2 copy.29
  425.6 0.2 copy.30
  425.9 1.7 fusion
  427.6 1.8 fusion.1
  429.4 3.3 divide_convert_fusion
  432.8 140.2 %all-gather.17.cloned.1.call-done = bf16[4096,1344]{0,1:T(8,128)(2,1)} async-done(((bf16[512,1344]{0,1:T(8,128)(2,1)}), bf16[4096,1344]{0,1:T(8,128)(2,1)}) %all-gather.17.cloned.1.call-update) | async-done | bytes 11010064 | tf_op jit(solution)/shard_map/all_gather | solution.py:126
  573.0 23.0 %all-gather.15.cloned.1.call-done = bf16[256,4096]{0,1:T(8,128)(2,1)} async-done(((bf16[256,1024]{0,1:T(8,128)(2,1)}), bf16[256,4096]{0,1:T(8,128)(2,1)}) %all-gather.15.cloned.1.call-update) | async-done | bytes 2097168 | tf_op jit(solution)/shard_map/all_gather | solution.py:123
  596.0 6.4 %multiply_reduce_fusion = (f32[256]{0:T(256)S(1)}, f32[256,1344]{0,1:T(8,128)S(1)}) fusion(bf16[4096,1344]{0,1:T(8,128)(2,1)} %all-gather.17.cloned.1.call-done, bf16[256,4096]{0,1:T(8,128)(2,1)} %all-gather.15.cloned.1.call-done), kind=kOutput, calls=%fused_computation.25 | convolution fusion | flops 2819260160 | bytes 14484480 | tf_op jit(solution)/shard_map/dot_general | solution.py:124
  602.4 5.3 psum.7
  607.7 1.2 add_convert_fusion
  (46 shorter events, 0.7 us)
Async XLA Ops:
  6.5 120.1 %copy-start.12 = (f32[5376]{0:T(1024)S(1)}, f32[5376]{0:T(1024)}, u32[]{:S(2)}) copy-start(f32[5376]{0:T(1024)} %param.13) | copy-start | bytes 64516
  6.5 29.3 %all-gather.7.cloned.1.call-start = ((), (), s32[]{:S(2)}) async-start(), calls=%async_computation | async-start | bytes 3440640 | tf_op jit(solution)/shard_map/all_gather | solution.py:60
  7.3 119.4 %all-gather.9.cloned.1.call-start = ((), (), s32[]{:S(2)}) async-start(), calls=%async_computation.1 | async-start | bytes 6193152 | tf_op jit(solution)/shard_map/all_gather | solution.py:66
  8.0 208.5 %all-gather.11.cloned.1.call-start = ((), (), s32[]{:S(2)}) async-start(), calls=%async_computation.2 | async-start | bytes 6193152 | tf_op jit(solution)/shard_map/all_gather | solution.py:67
  8.7 406.9 %all-gather.13.cloned.1.call-start = ((), (), s32[]{:S(2)}) async-start(), calls=%async_computation.3 | async-start | bytes 12386304 | tf_op jit(solution)/shard_map/all_gather | solution.py:68
  9.3 563.6 %all-gather.17.cloned.1.call-start = ((), (), s32[]{:S(2)}) async-start(), calls=%async_computation.5 | async-start | bytes 12386304 | tf_op jit(solution)/shard_map/all_gather | solution.py:126
  9.9 586.1 %all-gather.15.cloned.1.call-start = ((), (), s32[]{:S(2)}) async-start(), calls=%async_computation.4 | async-start | bytes 2621440 | tf_op jit(solution)/shard_map/all_gather | solution.py:123
  11.2 124.9 %copy-start.3 = (f32[256,64]{1,0:T(8,128)}, f32[256,64]{1,0:T(8,128)S(1)}, u32[]{:S(2)}) copy-start(f32[256,64]{1,0:T(8,128)S(1)} %get-tuple-element.11) | copy-start | bytes 196612
  11.2 124.9 %copy-start.5 = (f32[256,64]{1,0:T(8,128)}, f32[256,64]{1,0:T(8,128)S(1)}, u32[]{:S(2)}) copy-start(f32[256,64]{1,0:T(8,128)S(1)} %get-tuple-element.12) | copy-start | bytes 196612
  38.3 97.4 %copy-start.10 = (f32[128]{0:T(128)S(1)}, f32[128]{0:T(128)}, u32[]{:S(2)}) copy-start(f32[128]{0:T(128)} %param.18) | copy-start | bytes 1540
  134.0 82.6 %copy-start = (bf16[256,5376]{0,1:T(8,128)(2,1)S(1)}, bf16[256,5376]{0,1:T(8,128)(2,1)}, u32[]{:S(2)}) copy-start(bf16[256,5376]{0,1:T(8,128)(2,1)} %all-gather.7.cloned.1.call-done) | copy-start | bytes 8257540
  222.3 0.7 copy-start.7
  223.0 105.7 %copy-start.8 = (bf16[1,256,512]{2,1,0:T(8,128)(2,1)S(1)}, bf16[1,256,512]{2,1,0:T(8,128)(2,1)}, u32[]{:S(2)}) copy-start(bf16[1,256,512]{2,1,0:T(8,128)(2,1)} %copy-done.7) | copy-start | bytes 786436
  223.0 30.4 %collective-permute-start = (bf16[2,256,512]{2,1,0:T(8,128)(2,1)S(1)}, bf16[2,256,512]{2,1,0:T(8,128)(2,1)S(1)}, u32[]{:S(2)}, u32[]{:S(2)}) collective-permute-start(bf16[2,256,512]{2,1,0:T(8,128)(2,1)S(1)} %pad_maximum_fusion), channel_id=1, source_target_pairs={{0,1},{1,2},{2,3},{3,4},{4,5},{5,6},{6,7},{8,9},{9,10},{10,11},{11... | collective-permute-start | bytes 1572872 | tf_op jit(solution)/shard_map/ppermute | solution.py:18
  253.4 34.0 %collective-permute-start.1 = (bf16[2,256,512]{2,1,0:T(8,128)(2,1)S(1)}, bf16[2,256,512]{2,1,0:T(8,128)(2,1)S(1)}, u32[]{:S(2)}, u32[]{:S(2)}) collective-permute-start(bf16[2,256,512]{2,1,0:T(8,128)(2,1)S(1)} %collective-permute-done), channel_id=1, source_target_pairs={{0,1},{1,2},{2,3},{3,4},{4,5},{5,6},{6,7},{8,9},{9,10},{10,11},{11... | collective-permute-start | bytes 1572872 | tf_op jit(solution)/shard_map/ppermute | solution.py:18
  287.4 16.3 %collective-permute-start.2 = (bf16[2,256,512]{2,1,0:T(8,128)(2,1)S(1)}, bf16[2,256,512]{2,1,0:T(8,128)(2,1)S(1)}, u32[]{:S(2)}, u32[]{:S(2)}) collective-permute-start(bf16[2,256,512]{2,1,0:T(8,128)(2,1)S(1)} %collective-permute-done.1), channel_id=1, source_target_pairs={{0,1},{1,2},{2,3},{3,4},{4,5},{5,6},{6,7},{8,9},{9,10},{10,11},{11... | collective-permute-start | bytes 1572872 | tf_op jit(solution)/shard_map/ppermute | solution.py:18
  303.7 20.4 %collective-permute-start.3 = (bf16[2,256,512]{2,1,0:T(8,128)(2,1)S(1)}, bf16[2,256,512]{2,1,0:T(8,128)(2,1)S(1)}, u32[]{:S(2)}, u32[]{:S(2)}) collective-permute-start(bf16[2,256,512]{2,1,0:T(8,128)(2,1)S(1)} %collective-permute-done.2), channel_id=1, source_target_pairs={{0,1},{1,2},{2,3},{3,4},{4,5},{5,6},{6,7},{8,9},{9,10},{10,11},{11... | collective-permute-start | bytes 1572872 | tf_op jit(solution)/shard_map/ppermute | solution.py:18
  328.9 86.7 %copy-start.13 = (f32[5376]{0:T(1024)S(1)}, f32[5376]{0:T(1024)}, u32[]{:S(2)}) copy-start(f32[5376]{0:T(1024)} %param.13) | copy-start | bytes 64516
  334.3 90.2 %copy-start.11 = (f32[128]{0:T(128)S(1)}, f32[128]{0:T(128)}, u32[]{:S(2)}) copy-start(f32[128]{0:T(128)} %param.17) | copy-start | bytes 1540
  423.7 1.1 copy-start.4
  423.7 1.1 copy-start.6
  427.6 1.8 copy-start.2
  432.7 175.0 %copy-start.1 = (bf16[256,1344]{0,1:T(8,128)(2,1)S(1)}, bf16[256,1344]{0,1:T(8,128)(2,1)}, u32[]{:S(2)}) copy-start(bf16[256,1344]{0,1:T(8,128)(2,1)} %param.12) | copy-start | bytes 2064388
  432.8 175.0 %copy-start.9 = (f32[1344]{0:T(1024)S(1)}, f32[1344]{0:T(1024)}, u32[]{:S(2)}) copy-start(f32[1344]{0:T(1024)} %param.23) | copy-start | bytes 16132
Sparse Core Ops, SparseCore 0:
  8.9 26.8 all-gather.6
  38.0 88.6 all-gather.8
  128.9 87.6 all-gather.10
  218.6 196.9 all-gather.12
  417.5 155.4 all-gather.16
  574.4 21.5 all-gather.14
where the time goes:
time: 619 us; the launch traced here: 616 us
  waiting for transfers between devices  524 us (85%)
  matrix products  32.6 us (5%)
  starting transfers between devices  17.2 us (3%)
  between operations  14.5 us (2%)
  other arithmetic  14 us (2%)
  local copies, waits for them, and re-layouts  8.43 us (1%)
    all_gather x1, waiting for transfers between devices, on_device(): lax.all_gather(w_out, 'seq', axis=0, tiled=True)  140 us
    all_gather x1, waiting for transfers between devices, on_device(): keys_raw = add_rows(lax.all_gather(key_weight, 'seq', axis=0, tiled=True))  88.3 us
    ppermute x4, waiting for transfers between devices, shifted(): return lax.ppermute(x, axis, pairs)  83.7 us
    all_gather x1, waiting for transfers between devices, on_device(): query_matrix = add_rows(lax.all_gather(w_query, 'seq', axis=0, tiled=True))  81.3 us
    all_gather x1, waiting for transfers between devices, on_device(): lax.all_gather(value_weight, 'seq', axis=0, tiled=True)  79.4 us
    all_gather x1, waiting for transfers between devices, on_device(): full_rows = lax.all_gather(hidden_in, 'mp', axis=1, tiled=True)  24.6 us
    all_gather x1, waiting for transfers between devices, on_device(): all_heads = lax.all_gather(attn, 'mp', axis=1, tiled=True)  23 us
    dot_general x3, matrix products, add_rows(): jnp.dot(normed_hidden, block_rows, preferred_element_type=jnp.float32)  21.1 us
  transfers between devices with their start and end apart: 10, of which 10 were waited for; matrix products, arithmetic and copies ran while one was open for 8% of the time, Pallas kernels for 0%

commit v1 on v0

--- a/solution.py
+++ b/solution.py
@@ -1,6 +1,10 @@
+import functools
+
 import jax
 import jax.numpy as jnp
 from jax import lax
+from jax.experimental import pallas as pl
+from jax.experimental.pallas import tpu as pltpu
 from jax.sharding import PartitionSpec as P
 
 MODEL_WIDTH = 5376
@@ -10,6 +14,365 @@
 epsilon = 1e-06
 query_scale = 168.0 ** (-0.5)
 rope_base = 10000.0
+
+MESH = pl.DeviceIdType.MESH
+f32 = jnp.float32
+bf16 = jnp.bfloat16
+
+
+def layer_kernel(
+    hidden, gain_in, wq, wk, wv, gain_q, gain_k, cos_t, sin_t, cache_k, cache_v, wo, gain_post,
+    out,
+    xb, wb, ob, kv, qb, ab, rb, sb, ss,
+    local_sem, xz_send, xz_recv, xx_send, xx_recv, xc_send, xc_recv,
+    wz_send, wz_recv, wy_send, wy_recv, oz_send, oz_recv, oy_send, oy_recv,
+    kv_send, kv_recv, a_send, a_recv, r_send, r_recv, s_send, s_recv,
+):
+    NZ, NM = 4, 4
+    rows, cols = hidden.shape
+    depth = wq.shape[0]
+    m = lax.axis_index("mp")
+    s = lax.axis_index("seq")
+    z, y = s // 2, s % 2
+    x, c = m // 2, m % 2
+    ypeer = {"mp": m, "seq": 2 * z + (1 - y)}
+    xpeer_m = (1 - x) * 2 + c
+    cpeer_m = x * 2 + (1 - c)
+    xpeer = {"mp": xpeer_m, "seq": s}
+    cpeer = {"mp": cpeer_m, "seq": s}
+    head = (z + 4 - m) % 4
+
+    def at_z(zz):
+        return {"mp": m, "seq": 2 * zz + y}
+
+    def remote(src, dst, send, recv, dev):
+        return pltpu.make_async_remote_copy(
+            src_ref=src, dst_ref=dst, send_sem=send, recv_sem=recv,
+            device_id=dev, device_id_type=MESH)
+
+    barrier = pltpu.get_barrier_semaphore()
+    for d in range(1, 4):
+        pl.semaphore_signal(barrier, inc=1, device_id=at_z((z + d) % 4), device_id_type=MESH)
+        pl.semaphore_signal(barrier, inc=1, device_id={"mp": (m + d) % 4, "seq": s}, device_id_type=MESH)
+    pl.semaphore_signal(barrier, inc=1, device_id=ypeer, device_id_type=MESH)
+
+    k_own = head
+    locals_ = [
+        (None, pltpu.make_async_copy(hidden, xb.at[z, m], local_sem.at[0])),
+        (None, pltpu.make_async_copy(cache_k.at[:, pl.ds(pl.multiple_of(head * 128, 128), 128)], kv.at[pl.ds(0, 1024), pl.ds(0, 128)], local_sem.at[1])),
+        (None, pltpu.make_async_copy(cache_v.at[:, pl.ds(pl.multiple_of(head * 128, 128), 128)], kv.at[pl.ds(0, 1024), pl.ds(128, 128)], local_sem.at[2])),
+    ]
+
+    def w_parts(k, zsrc):
+        r0 = pl.ds(pl.multiple_of(y * depth, 16), depth)
+        return [
+            (wq.at[:, pl.ds(pl.multiple_of(k * 256, 128), 256)], wb.at[zsrc, r0, pl.ds(0, 256)]),
+            (wk.at[:, pl.ds(pl.multiple_of(k * 128, 128), 128)], wb.at[zsrc, r0, pl.ds(256, 128)]),
+            (wv.at[:, pl.ds(pl.multiple_of(k * 128, 128), 128)], wb.at[zsrc, r0, pl.ds(384, 128)]),
+        ]
+
+    for i, (a, b) in enumerate(w_parts(k_own, z)):
+        locals_.append((None, pltpu.make_async_copy(a, b, local_sem.at[3 + i])))
+    o_half = []
+    for h in range(2):
+        zd = (2 * y + h + z) % 4
+        o_half.append((zd, wo.at[pl.ds(h * 256, 256), :], ob.at[z]))
+        cp = pltpu.make_async_copy(wo.at[pl.ds(h * 256, 256), :], ob.at[z], local_sem.at[6])
+        locals_.append((zd == z, cp))
+
+    def when(cond, fn):
+        if cond is None:
+            fn()
+        else:
+            pl.when(cond)(fn)
+
+    for cond, cp in locals_:
+        when(cond, cp.start)
+
+    pl.semaphore_wait(barrier, 7)
+
+    pending = []
+
+    def send(cond, cp):
+        when(cond, cp.start)
+        pending.append((cond, cp))
+
+    def x_right(zz):
+        return remote(xb.at[zz, m], xb.at[zz, m], xz_send.at[0, zz], xz_recv.at[zz], at_z((z + 1) % 4))
+
+    def x_left(zz):
+        return remote(xb.at[zz, m], xb.at[zz, m], xz_send.at[1, zz], xz_recv.at[zz], at_z((z + 3) % 4))
+
+    def x_x(zz):
+        return remote(xb.at[zz, m], xb.at[zz, m], xx_send.at[zz], xx_recv.at[zz], xpeer)
+
+    def x_c(zz, mm, which):
+        return remote(xb.at[zz, mm], xb.at[zz, mm], xc_send.at[which, zz], xc_recv.at[which, zz], cpeer)
+
+    locals_[0][1].wait()
+    send(z < 3, x_right(z))
+    send(z > 0, x_left(z))
+    for d in (2, 1, 3):
+        zd = (z + d) % 4
+        k = (zd + 4 - m) % 4
+        for i, (a, b) in enumerate(w_parts(k, z)):
+            send(None, remote(a, b, wz_send.at[d, i], wz_recv.at[z, i], at_z(zd)))
+    send(None, x_x(z))
+    send(None, x_c(z, m, 0))
+    for h in range(2):
+        zd, a, b = o_half[h]
+        send(zd != z, remote(a, b, oz_send.at[h], oz_recv.at[z], at_z(zd)))
+
+    def w_forward(zsrc, sem):
+        r0 = pl.ds(pl.multiple_of(y * depth, 16), depth)
+        return remote(wb.at[zsrc, r0, :], wb.at[zsrc, r0, :], wy_send.at[sem], wy_recv.at[zsrc], ypeer)
+
+    for i in range(3):
+        locals_[3 + i][1].wait()
+    send(None, w_forward(z, 0))
+
+    def x_from(cond, zz):
+        def arrived():
+            x_right(zz).wait_recv()
+        when(cond, arrived)
+
+    def x_from_x(cond, zz):
+        def arrived():
+            x_x(zz).wait_recv()
+        when(cond, arrived)
+        send(cond, x_c(zz, xpeer_m, 1))
+
+    x_from_x(None, z)
+    for d in range(1, 4):
+        left, right = z - d, z + d
+        lz, rz = (z + 4 - d) % 4, (z + d) % 4
+        x_from(left >= 0, lz)
+        send((left >= 0) & (z < 3), x_right(lz))
+        send(left >= 0, x_x(lz))
+        send(left >= 0, x_c(lz, m, 0))
+        x_from(right <= 3, rz)
+        send((right <= 3) & (z > 0), x_left(rz))
+        send(right <= 3, x_x(rz))
+        send(right <= 3, x_c(rz, m, 0))
+        zs = (z + 4 - d) % 4
+        for i, (a, b) in enumerate(w_parts(0, zs)):
+            remote(b, b, wz_send.at[0, i], wz_recv.at[zs, i], ypeer).wait_recv()
+        send(None, w_forward(zs, d))
+        x_from_x(left >= 0, lz)
+        x_from_x(right <= 3, rz)
+
+    for zs in range(4):
+        mine = ((z + 4 - zs) % 4) // 2 == y
+        own = zs == z
+        ow = remote(ob.at[zs], ob.at[zs], oz_send.at[0], oz_recv.at[zs], ypeer)
+        when(mine & (zs != z), ow.wait_recv)
+        when(mine & own, pltpu.make_async_copy(ob.at[zs], ob.at[zs], local_sem.at[6]).wait)
+        send(mine, remote(ob.at[zs], ob.at[zs], oy_send.at[zs], oy_recv.at[zs], ypeer))
+
+    for zs in range(4):
+        for which in range(2):
+            mm = cpeer_m if which == 0 else (1 - x) * 2 + (1 - c)
+            remote(xb.at[zs, mm], xb.at[zs, mm], xc_send.at[which, zs], xc_recv.at[which, zs], cpeer).wait_recv()
+        r1 = pl.ds(pl.multiple_of((1 - y) * depth, 16), depth)
+        remote(wb.at[zs, r1, :], wb.at[zs, r1, :], wy_send.at[zs], wy_recv.at[zs], ypeer).wait_recv()
+
+    def kv_copy(b):
+        r = pl.ds(pl.multiple_of(1024 + (2 * b + y) * 256, 256), 256)
+        return remote(kv.at[r, :], kv.at[r, :], kv_send.at[b], kv_recv.at[b], ypeer)
+
+    def head_norm(g, gain, cosine, sine):
+        g = g * lax.rsqrt(jnp.mean(g * g, axis=-1, keepdims=True) + epsilon) * gain
+        return g * cosine + pltpu.roll(g, 64, 1) * sine
+
+    def project(b, carry):
+        total = jnp.zeros((rows, 1), f32)
+        for mm in range(NM):
+            v = xb[b, mm].astype(f32)
+            total += jnp.sum(v * v, axis=-1, keepdims=True)
+        scale = lax.rsqrt(total / MODEL_WIDTH + epsilon)
+        acc = jnp.zeros((rows, 512), f32)
+        for mm in range(NM):
+            n = (xb[b, mm].astype(f32) * scale * gain_in[mm]).astype(bf16)
+            acc += jnp.dot(n, wb[mm], preferred_element_type=f32)
+        r = pl.ds(pl.multiple_of(b * rows, rows), rows)
+        cosine, sine = cos_t[r, :], sin_t[r, :]
+        for h in range(2):
+            q = head_norm(acc[:, h * 128:(h + 1) * 128], gain_q[...], cosine, sine) * query_scale
+            qb[h, r, :] = q.astype(bf16)
+        rk = pl.ds(pl.multiple_of(1024 + (2 * b + y) * 256, 256), 256)
+        kv[rk, 0:128] = head_norm(acc[:, 256:384], gain_k[...], cosine, sine).astype(bf16)
+        kv[rk, 128:256] = acc[:, 384:512].astype(bf16)
+        kv_copy(b).start()
+        return carry
+
+    lax.fori_loop(0, NZ, project, 0)
+    locals_[1][1].wait()
+    locals_[2][1].wait()
+
+    def kv_wait(b, carry):
+        r = pl.ds(pl.multiple_of(1024 + (2 * b + (1 - y)) * 256, 256), 256)
+        remote(kv.at[r, :], kv.at[r, :], kv_send.at[b], kv_recv.at[b], ypeer).wait_recv()
+        kv_copy(b).wait_send()
+        return carry
+
+    lax.fori_loop(0, NZ, kv_wait, 0)
+
+    def a_copy(b, d):
+        r = pl.ds(pl.multiple_of(b * rows, rows), rows)
+        return remote(ab.at[m, r, :], ab.at[m, r, :], a_send.at[b, d], a_recv.at[b, m],
+                      {"mp": (m + d) % 4, "seq": s})
+
+    def attend(b, carry):
+        r = pl.ds(pl.multiple_of(b * rows, rows), rows)
+        span = WINDOW_LENGTH + 256
+        rk = pl.ds(pl.multiple_of((2 * b + y) * 256, 256), span)
+        keys = kv[rk, 0:128]
+        vals = kv[rk, 128:256]
+        qi = lax.broadcasted_iota(jnp.int32, (rows, span), 0)
+        ei = lax.broadcasted_iota(jnp.int32, (rows, span), 1)
+        visible = (ei > qi) & (ei <= qi + WINDOW_LENGTH)
+        for h in range(2):
+            sc = lax.dot_general(qb[h, r, :], keys, (((1,), (1,)), ((), ())), preferred_element_type=f32)
+            sc = jnp.where(visible, sc, -jnp.inf)
+            top = jnp.max(sc, axis=-1, keepdims=True)
+            p = jnp.exp(sc - top)
+            tot = jnp.sum(p, axis=-1, keepdims=True)
+            o = jnp.dot(p.astype(bf16), vals, preferred_element_type=f32)
+            ab[m, r, h * 128:(h + 1) * 128] = (o / tot).astype(bf16)
+        for d in range(1, 4):
+            a_copy(b, d).start()
+        return carry
+
+    lax.fori_loop(0, NZ, attend, 0)
+
+    for zs in range(4):
+        other = ((z + 4 - zs) % 4) // 2 != y
+        when(other, remote(ob.at[zs], ob.at[zs], oy_send.at[zs], oy_recv.at[zs], ypeer).wait_recv)
+
+    def a_wait(b, carry):
+        r = pl.ds(pl.multiple_of(b * rows, rows), rows)
+        for d in range(1, 4):
+            mm = (m + d) % 4
+            remote(ab.at[mm, r, :], ab.at[mm, r, :], a_send.at[b, d], a_recv.at[b, mm], ypeer).wait_recv()
+            a_copy(b, d).wait_send()
+        return carry
+
+    lax.fori_loop(0, NZ, a_wait, 0)
+
+    def partial(b):
+        r = pl.ds(pl.multiple_of(b * rows, rows), rows)
+        acc = jnp.dot(ab[0, r, :], ob[0], preferred_element_type=f32)
+        for mm in range(1, NM):
+            acc += jnp.dot(ab[mm, r, :], ob[mm], preferred_element_type=f32)
+        return acc
+
+    def r_copy(side, d, zd):
+        return remote(sb.at[d], rb.at[side, d], r_send.at[d], r_recv.at[side, d], at_z(zd))
+
+    def hop(side, d, inner):
+        def go():
+            sb[d] = partial(d).astype(bf16)
+
+            def add():
+                r_copy(side, d, z).wait_recv()
+                sb[d] = (partial(d) + rb[side, d].astype(f32)).astype(bf16)
+            pl.when(inner)(add)
+            r_copy(side, d, (z + 1) % 4 if side == 0 else (z + 3) % 4).start()
+        return go
+
+    for i in range(3):
+        dr, dl = 3 - i, i
+        pl.when(z < dr)(hop(0, dr, z > 0))
+        pl.when(z > dl)(hop(1, dl, z < 3))
+
+    out_acc = xb.shape and partial(z)
+    ss_acc = out_acc
+    zero = jnp.zeros_like(out_acc)
+
+    @pl.when(z > 0)
+    def _():
+        r_copy(0, z, (z + 1) % 4).wait_recv()
+
+    @pl.when(z == 0)
+    def _():
+        rb[0, z] = zero.astype(bf16)
+
+    @pl.when(z < 3)
+    def _():
+        r_copy(1, z, (z + 1) % 4).wait_recv()
+
+    @pl.when(z == 3)
+    def _():
+        rb[1, z] = zero.astype(bf16)
+
+    mixed = ss_acc + rb[0, z].astype(f32) + rb[1, z].astype(f32)
+    ss[m] = jnp.broadcast_to(jnp.sum(mixed * mixed, axis=-1, keepdims=True), (rows, 128))
+
+    def s_copy(d):
+        return remote(ss.at[m], ss.at[m], s_send.at[d], s_recv.at[m], {"mp": (m + d) % 4, "seq": s})
+
+    for d in range(1, 4):
+        s_copy(d).start()
+    for d in range(1, 4):
+        mm = (m + d) % 4
+        remote(ss.at[mm], ss.at[mm], s_send.at[d], s_recv.at[mm], ypeer).wait_recv()
+    squares = (ss[0] + ss[1] + ss[2] + ss[3])[:, 0:1]
+    scaling = lax.rsqrt(squares / MODEL_WIDTH + epsilon)
+    out[...] = (xb[z, m].astype(f32) + mixed * scaling * gain_post[...]).astype(bf16)
+
+    for d in range(1, 4):
+        s_copy(d).wait_send()
+    for d in range(4):
+        when(z != d, r_copy(0, d, (z + 1) % 4).wait_send)
+    for cond, cp in pending:
+        when(cond, cp.wait_send)
+
+
+def fused(
+    hidden_in, gain_in, w_query, key_weight, value_weight, gain_query, gain_key, start_pos,
+    cached_key_rows, cached_value_rows, w_out, gain_post,
+):
+    rows, cols = hidden_in.shape
+    depth = w_query.shape[0]
+    y = lax.axis_index("seq") % 2
+    block = jnp.arange(4, dtype=jnp.int32)[:, None] * 2 + y
+    positions = (start_pos[0] + block * rows + jnp.arange(rows, dtype=jnp.int32)[None, :]).reshape(-1)
+    inverse_freq = rope_base ** (-(jnp.arange(64, dtype=f32) * 2.0) / 128)
+    angles = positions.astype(f32)[:, None] * inverse_freq[None, :]
+    cosine, sine = jnp.cos(angles), jnp.sin(angles)
+    cos_t = jnp.concatenate([cosine, cosine], axis=1)
+    sin_t = jnp.concatenate([-sine, sine], axis=1)
+    hbm = pl.BlockSpec(memory_space=pl.ANY)
+    vmem = pl.BlockSpec(memory_space=pltpu.VMEM)
+    dma = pltpu.SemaphoreType.DMA
+    return pl.pallas_call(
+        layer_kernel,
+        name="layer",
+        out_shape=jax.ShapeDtypeStruct((rows, cols), bf16),
+        in_specs=[hbm, vmem, hbm, hbm, hbm, vmem, vmem, vmem, vmem, hbm, hbm, hbm, vmem],
+        out_specs=vmem,
+        scratch_shapes=[
+            pltpu.VMEM((4, 4, rows, cols), bf16),
+            pltpu.VMEM((4, 2 * depth, 512), bf16),
+            pltpu.VMEM((4, 256, cols), bf16),
+            pltpu.VMEM((3072, 256), bf16),
+            pltpu.VMEM((2, 1024, 128), bf16),
+            pltpu.VMEM((4, 1024, 256), bf16),
+            pltpu.VMEM((2, 4, rows, cols), bf16),
+            pltpu.VMEM((4, rows, cols), bf16),
+            pltpu.VMEM((4, rows, 128), f32),
+            dma((7,)), dma((2, 4)), dma((4,)), dma((4,)), dma((4,)), dma((2, 4)), dma((2, 4)),
+            dma((4, 3)), dma((4, 3)), dma((4,)), dma((4,)), dma((2,)), dma((4,)), dma((4,)), dma((4,)),
+            dma((4,)), dma((4,)), dma((4, 4)), dma((4, 4)), dma((4,)), dma((2, 4)), dma((4,)), dma((4,)),
+        ],
+        compiler_params=pltpu.CompilerParams(
+            collective_id=0, has_side_effects=True, vmem_limit_bytes=56 * 1024 * 1024,
+        ),
+    )(
+        hidden_in, gain_in.reshape(4, 1, cols), w_query, key_weight, value_weight,
+        gain_query.reshape(1, 128), gain_key.reshape(1, 128), cos_t, sin_t,
+        cached_key_rows, cached_value_rows, w_out, gain_post.reshape(1, cols),
+    )
 
 
 def shifted(x, axis, by):
@@ -149,6 +512,7 @@
         P("mp"),
     )
     out_specs = P("seq", "mp")
+    fits = mesh.shape["mp"] == 4 and mesh.shape["seq"] == 8
     return jax.shard_map(
-        on_device, mesh=mesh, in_specs=in_specs, out_specs=out_specs, check_vma=False
-    )
+        fused if fits else on_device, mesh=mesh, in_specs=in_specs, out_specs=out_specs, check_vma=False
+    )

time: 619 us -> 336 us (0.54)
  waiting for transfers between devices: 524 us -> 0 us
  Pallas kernels: 0 us -> 326 us
  matrix products: 32.6 us -> 0 us
  starting transfers between devices: 17.2 us -> 0 us
  between operations: 14.5 us -> 0.69 us
  other arithmetic: 14 us -> 3.3 us
    all_gather x6 -> x0, waiting for transfers between devices: 437 us -> none  [the longest x1 140 us: on_device(): lax.all_gather(w_out, 'seq', axis=0, tiled=True)]
    pallas_call x0 -> x1, Pallas kernels: none -> 326 us  [fused(): pl.pallas_call(layer_kernel, name='layer', out_shape=jax.ShapeDtypeStruct...]
    ppermute x4 -> x0, waiting for transfers between devices: 83.7 us -> none  [shifted(): return lax.ppermute(x, axis, pairs)]
    dot_general x6 -> x0, matrix products: 32.6 us -> none  [the longest x3 21.1 us: add_rows(): jnp.dot(normed_hidden, block_rows, preferred_element_type=jnp.float32)]
    ppermute x4 -> x0, starting transfers between devices: 17 us -> none  [shifted(): return lax.ppermute(x, axis, pairs)]
  transfers between devices with their start and end apart: 10 -> 0, of which waited for: 10 -> 0; matrix products, arithmetic and copies ran while one was open for 8% -> 0% of each run, Pallas kernels for 0% -> 0%
where the time goes in v1:
time: 336 us
  Pallas kernels  326 us (97%)
  local copies, waits for them, and re-layouts  6.33 us (2%)
    pallas_call x1, Pallas kernels, fused(): pl.pallas_call(layer_kernel, name='layer', out_shape=jax.ShapeDtypeStruct...  326 us

profile of v1, /device:TPU:19, one launch (start us, length us, event | category | flops | bytes accessed | tf_op | source)
XLA Modules:
  0.0 336.1 jit_solution(17474384825685260146)
XLA Ops:
  0.7 0.1 convert_bitcast_fusion
  0.8 1.9 fusion
  2.7 0.0 copy-start
  2.7 1.3 pad_maximum_fusion
  4.0 0.1 copy-done
  4.1 0.0 copy-start.1
  4.1 1.5 copy.14.wo
  5.7 0.0 copy-done.1
  5.7 0.0 copy-start.2
  5.7 0.0 copy-start.3
  5.7 1.1 copy.13.hidden
  6.8 0.0 copy-done.2
  6.8 0.7 reshape.45.gain_in
  7.5 0.0 copy-done.3
  7.5 0.6 reshape.48.gain_post
  8.1 325.7 %layer.1 = bf16[256,1344]{1,0:T(8,128)(2,1)} custom-call(bf16[256,1344]{1,0:T(8,128)(2,1)} %copy.13.hidden, f32[4,1,1344]{2,1,0:T(1,128)} %reshape.45.gain_in, bf16[672,1024]{1,0:T(8,128)(2,1)} %wq.1, bf16[672,512]{1,0:T(8,128)(2,1)} %wk.1, bf16[672,512]{1,0:T(8,128)(2,1)} %wv.1, f32[1,128]{1,0:T(1,128)} %bitcast.8, f32[1,128]{1,0:T(1,128)} %bitcast.9, ...), custom_call_target="tpu_custom_call" | custom-call | tf_op jit(solution)/shard_map/layer/pallas_call | solution.py:348
  333.9 2.2 copy.15
  (3 shorter events, 0.0 us)
Async XLA Ops:
  2.7 1.5 copy-start
  4.1 1.5 copy-start.1
  5.7 1.1 copy-start.2
  5.7 1.8 copy-start.3

commit v2 on v1

--- a/solution.py
+++ b/solution.py
@@ -23,9 +23,9 @@
 def layer_kernel(
     hidden, gain_in, wq, wk, wv, gain_q, gain_k, cos_t, sin_t, cache_k, cache_v, wo, gain_post,
     out,
-    xb, wb, ob, kv, qb, ab, rb, sb, ss,
+    xb, xn, tb, wb, ob, kv, qb, ab, rb, sb, ss, pacc,
     local_sem, xz_send, xz_recv, xx_send, xx_recv, xc_send, xc_recv,
-    wz_send, wz_recv, wy_send, wy_recv, oz_send, oz_recv, oy_send, oy_recv,
+    t_send, t_recv, wz_send, wz_recv, wy_send, wy_recv, c_send, c_recv, oy_send, oy_recv,
     kv_send, kv_recv, a_send, a_recv, r_send, r_recv, s_send, s_recv,
 ):
     NZ, NM = 4, 4
@@ -40,7 +40,6 @@
     cpeer_m = x * 2 + (1 - c)
     xpeer = {"mp": xpeer_m, "seq": s}
     cpeer = {"mp": cpeer_m, "seq": s}
-    head = (z + 4 - m) % 4
 
     def at_z(zz):
         return {"mp": m, "seq": 2 * zz + y}
@@ -56,29 +55,35 @@
         pl.semaphore_signal(barrier, inc=1, device_id={"mp": (m + d) % 4, "seq": s}, device_id_type=MESH)
     pl.semaphore_signal(barrier, inc=1, device_id=ypeer, device_id_type=MESH)
 
-    k_own = head
-    locals_ = [
-        (None, pltpu.make_async_copy(hidden, xb.at[z, m], local_sem.at[0])),
-        (None, pltpu.make_async_copy(cache_k.at[:, pl.ds(pl.multiple_of(head * 128, 128), 128)], kv.at[pl.ds(0, 1024), pl.ds(0, 128)], local_sem.at[1])),
-        (None, pltpu.make_async_copy(cache_v.at[:, pl.ds(pl.multiple_of(head * 128, 128), 128)], kv.at[pl.ds(0, 1024), pl.ds(128, 128)], local_sem.at[2])),
+    def w_parts(j, k):
+        return [
+            (wq.at[:, pl.ds(pl.multiple_of(j * 256, 128), 256)], tb.at[k, :, pl.ds(0, 256)]),
+            (wk.at[:, pl.ds(pl.multiple_of(j * 128, 128), 128)], tb.at[k, :, pl.ds(256, 128)]),
+            (wv.at[:, pl.ds(pl.multiple_of(j * 128, 128), 128)], tb.at[k, :, pl.ds(384, 128)]),
+        ]
+
+    def wb_at(zsrc, yy):
+        return wb.at[zsrc, pl.ds(pl.multiple_of(yy * depth, 16), depth), :]
+
+    def c_parts(j):
+        return [
+            (cache_k.at[:, pl.ds(j * 128, 128)], kv.at[pl.ds(0, 1024), pl.ds(0, 128)]),
+            (cache_v.at[:, pl.ds(j * 128, 128)], kv.at[pl.ds(0, 1024), pl.ds(128, 128)]),
+        ]
+
+    locals_ = [(None, pltpu.make_async_copy(hidden, xb.at[z, m], local_sem.at[0]))]
+    own_w = [
+        (None, pltpu.make_async_copy(a, b, local_sem.at[1 + i])) for i, (a, b) in enumerate(w_parts(m, m))
     ]
-
-    def w_parts(k, zsrc):
-        r0 = pl.ds(pl.multiple_of(y * depth, 16), depth)
-        return [
-            (wq.at[:, pl.ds(pl.multiple_of(k * 256, 128), 256)], wb.at[zsrc, r0, pl.ds(0, 256)]),
-            (wk.at[:, pl.ds(pl.multiple_of(k * 128, 128), 128)], wb.at[zsrc, r0, pl.ds(256, 128)]),
-            (wv.at[:, pl.ds(pl.multiple_of(k * 128, 128), 128)], wb.at[zsrc, r0, pl.ds(384, 128)]),
-        ]
-
-    for i, (a, b) in enumerate(w_parts(k_own, z)):
-        locals_.append((None, pltpu.make_async_copy(a, b, local_sem.at[3 + i])))
-    o_half = []
-    for h in range(2):
-        zd = (2 * y + h + z) % 4
-        o_half.append((zd, wo.at[pl.ds(h * 256, 256), :], ob.at[z]))
-        cp = pltpu.make_async_copy(wo.at[pl.ds(h * 256, 256), :], ob.at[z], local_sem.at[6])
-        locals_.append((zd == z, cp))
+    own_c = []
+    for j in range(4):
+        mine = (m == j) & (z == j)
+        own_c.extend((mine, pltpu.make_async_copy(a, b, local_sem.at[4 + i])) for i, (a, b) in enumerate(c_parts(j)))
+    own_o = [
+        (None, pltpu.make_async_copy(wo.at[pl.ds(h * 256, 256), :], ob.at[2 * y + h], local_sem.at[6 + h]))
+        for h in range(2)
+    ]
+    locals_ = locals_ + own_w + own_c + own_o
 
     def when(cond, fn):
         if cond is None:
@@ -109,91 +114,112 @@
     def x_c(zz, mm, which):
         return remote(xb.at[zz, mm], xb.at[zz, mm], xc_send.at[which, zz], xc_recv.at[which, zz], cpeer)
 
+    def w_first(d):
+        j = (m + d) % 4
+        for i, (a, b) in enumerate(w_parts(j, m)):
+            send(None, remote(a, b, t_send.at[d, i], t_recv.at[m, i], {"mp": j, "seq": s}))
+
+    def w_second(k, d):
+        for i, (a, b) in enumerate(w_parts(m, k)):
+            remote(b, b, t_send.at[0, i], t_recv.at[k, i], ypeer).wait_recv()
+        w_along(k, d)
+
+    def w_along(k, d):
+        send(k != z, remote(tb.at[k], wb_at(z, y), wz_send.at[d], wz_recv.at[z], at_z(k)))
+        pl.when(k == z)(pltpu.make_async_copy(tb.at[k], wb_at(z, y), local_sem.at[8]).start)
+
+    def w_third(zs, d):
+        if d == 0:
+            pltpu.make_async_copy(tb.at[z], wb_at(z, y), local_sem.at[8]).wait()
+        else:
+            remote(tb.at[z], wb_at(zs, y), wz_send.at[0], wz_recv.at[zs], ypeer).wait_recv()
+        send(None, remote(wb_at(zs, y), wb_at(zs, y), wy_send.at[d], wy_recv.at[zs], ypeer))
+
     locals_[0][1].wait()
     send(z < 3, x_right(z))
     send(z > 0, x_left(z))
-    for d in (2, 1, 3):
-        zd = (z + d) % 4
-        k = (zd + 4 - m) % 4
-        for i, (a, b) in enumerate(w_parts(k, z)):
-            send(None, remote(a, b, wz_send.at[d, i], wz_recv.at[z, i], at_z(zd)))
+    w_first(2)
+    w_first(1)
+    w_first(3)
+    for h in range(2):
+        send(None, remote(wo.at[pl.ds(h * 256, 256), :], ob.at[2 * y + h], oy_send.at[h], oy_recv.at[h], ypeer))
+    for _, cp in own_w:
+        cp.wait()
+    w_along(m, 0)
+    send(None, x_c(z, m, 0))
     send(None, x_x(z))
-    send(None, x_c(z, m, 0))
-    for h in range(2):
-        zd, a, b = o_half[h]
-        send(zd != z, remote(a, b, oz_send.at[h], oz_recv.at[z], at_z(zd)))
-
-    def w_forward(zsrc, sem):
-        r0 = pl.ds(pl.multiple_of(y * depth, 16), depth)
-        return remote(wb.at[zsrc, r0, :], wb.at[zsrc, r0, :], wy_send.at[sem], wy_recv.at[zsrc], ypeer)
-
-    for i in range(3):
-        locals_[3 + i][1].wait()
-    send(None, w_forward(z, 0))
-
-    def x_from(cond, zz):
-        def arrived():
-            x_right(zz).wait_recv()
-        when(cond, arrived)
-
-    def x_from_x(cond, zz):
-        def arrived():
-            x_x(zz).wait_recv()
-        when(cond, arrived)
-        send(cond, x_c(zz, xpeer_m, 1))
-
-    x_from_x(None, z)
-    for d in range(1, 4):
+    w_second(cpeer_m, 1)
+
+    def x_step(d):
         left, right = z - d, z + d
         lz, rz = (z + 4 - d) % 4, (z + d) % 4
-        x_from(left >= 0, lz)
+        when(left >= 0, x_right(lz).wait_recv)
         send((left >= 0) & (z < 3), x_right(lz))
         send(left >= 0, x_x(lz))
         send(left >= 0, x_c(lz, m, 0))
-        x_from(right <= 3, rz)
+        when(right <= 3, x_right(rz).wait_recv)
         send((right <= 3) & (z > 0), x_left(rz))
         send(right <= 3, x_x(rz))
         send(right <= 3, x_c(rz, m, 0))
-        zs = (z + 4 - d) % 4
-        for i, (a, b) in enumerate(w_parts(0, zs)):
-            remote(b, b, wz_send.at[0, i], wz_recv.at[zs, i], ypeer).wait_recv()
-        send(None, w_forward(zs, d))
-        x_from_x(left >= 0, lz)
-        x_from_x(right <= 3, rz)
-
-    for zs in range(4):
-        mine = ((z + 4 - zs) % 4) // 2 == y
-        own = zs == z
-        ow = remote(ob.at[zs], ob.at[zs], oz_send.at[0], oz_recv.at[zs], ypeer)
-        when(mine & (zs != z), ow.wait_recv)
-        when(mine & own, pltpu.make_async_copy(ob.at[zs], ob.at[zs], local_sem.at[6]).wait)
-        send(mine, remote(ob.at[zs], ob.at[zs], oy_send.at[zs], oy_recv.at[zs], ypeer))
-
+
+    def x_cross(d):
+        left, right = z - d, z + d
+        if d == 0:
+            pairs = [(None, z)]
+        else:
+            pairs = [(left >= 0, (z + 4 - d) % 4), (right <= 3, (z + d) % 4)]
+        for cond, zz in pairs:
+            when(cond, x_x(zz).wait_recv)
+            send(cond, x_c(zz, xpeer_m, 1))
+
+    x_step(1)
+    w_second(xpeer_m, 2)
+    w_second((1 - x) * 2 + (1 - c), 3)
+    w_third(z, 0)
+    x_step(2)
+    x_cross(0)
+    w_third((z + 3) % 4, 1)
+    w_third((z + 1) % 4, 2)
+    x_step(3)
+    x_cross(1)
+    w_third((z + 2) % 4, 3)
+    x_cross(2)
+    x_cross(3)
+
+    for j in range(4):
+        for i, (a, b) in enumerate(c_parts(j)):
+            send((m == z) & (m != j), remote(a, b, c_send.at[j, i], c_recv.at[i], {"mp": j, "seq": s}))
     for zs in range(4):
         for which in range(2):
             mm = cpeer_m if which == 0 else (1 - x) * 2 + (1 - c)
             remote(xb.at[zs, mm], xb.at[zs, mm], xc_send.at[which, zs], xc_recv.at[which, zs], cpeer).wait_recv()
-        r1 = pl.ds(pl.multiple_of((1 - y) * depth, 16), depth)
-        remote(wb.at[zs, r1, :], wb.at[zs, r1, :], wy_send.at[zs], wy_recv.at[zs], ypeer).wait_recv()
-
-    def kv_copy(b):
-        r = pl.ds(pl.multiple_of(1024 + (2 * b + y) * 256, 256), 256)
-        return remote(kv.at[r, :], kv.at[r, :], kv_send.at[b], kv_recv.at[b], ypeer)
-
-    def head_norm(g, gain, cosine, sine):
-        g = g * lax.rsqrt(jnp.mean(g * g, axis=-1, keepdims=True) + epsilon) * gain
-        return g * cosine + pltpu.roll(g, 64, 1) * sine
-
-    def project(b, carry):
+
+    def norm_block(b, carry):
         total = jnp.zeros((rows, 1), f32)
         for mm in range(NM):
             v = xb[b, mm].astype(f32)
             total += jnp.sum(v * v, axis=-1, keepdims=True)
         scale = lax.rsqrt(total / MODEL_WIDTH + epsilon)
-        acc = jnp.zeros((rows, 512), f32)
         for mm in range(NM):
-            n = (xb[b, mm].astype(f32) * scale * gain_in[mm]).astype(bf16)
-            acc += jnp.dot(n, wb[mm], preferred_element_type=f32)
+            xn[b, mm] = (xb[b, mm].astype(f32) * scale * gain_in[mm]).astype(bf16)
+        return carry
+
+    lax.fori_loop(0, NZ, norm_block, 0)
+    for zs in range(4):
+        remote(wb_at(zs, 1 - y), wb_at(zs, 1 - y), wy_send.at[zs], wy_recv.at[zs], ypeer).wait_recv()
+
+    def kv_copy(b):
+        r = pl.ds(pl.multiple_of(1024 + (2 * b + y) * 256, 256), 256)
+        return remote(kv.at[r, :], kv.at[r, :], kv_send.at[b], kv_recv.at[b], ypeer)
+
+    def head_norm(g, gain, cosine, sine):
+        g = g * lax.rsqrt(jnp.mean(g * g, axis=-1, keepdims=True) + epsilon) * gain
+        return g * cosine + pltpu.roll(g, 64, 1) * sine
+
+    def project(b, carry):
+        acc = jnp.dot(xn[b, 0], wb[0], preferred_element_type=f32)
+        for mm in range(1, NM):
+            acc += jnp.dot(xn[b, mm], wb[mm], preferred_element_type=f32)
         r = pl.ds(pl.multiple_of(b * rows, rows), rows)
         cosine, sine = cos_t[r, :], sin_t[r, :]
         for h in range(2):
@@ -206,8 +232,9 @@
         return carry
 
     lax.fori_loop(0, NZ, project, 0)
-    locals_[1][1].wait()
-    locals_[2][1].wait()
+    for i, (a, b) in enumerate(c_parts(0)):
+        pl.when(m == z)(pltpu.make_async_copy(a, b, local_sem.at[4 + i]).wait)
+        pl.when(m != z)(remote(b, b, c_send.at[0, i], c_recv.at[i], ypeer).wait_recv)
 
     def kv_wait(b, carry):
         r = pl.ds(pl.multiple_of(1024 + (2 * b + (1 - y)) * 256, 256), 256)
@@ -222,15 +249,16 @@
         return remote(ab.at[m, r, :], ab.at[m, r, :], a_send.at[b, d], a_recv.at[b, m],
                       {"mp": (m + d) % 4, "seq": s})
 
-    def attend(b, carry):
+    span = WINDOW_LENGTH + 256
+    qi = lax.broadcasted_iota(jnp.int32, (rows, span), 0)
+    ei = lax.broadcasted_iota(jnp.int32, (rows, span), 1)
+    visible = (ei > qi) & (ei <= qi + WINDOW_LENGTH)
+
+    def attend(b):
         r = pl.ds(pl.multiple_of(b * rows, rows), rows)
-        span = WINDOW_LENGTH + 256
         rk = pl.ds(pl.multiple_of((2 * b + y) * 256, 256), span)
         keys = kv[rk, 0:128]
         vals = kv[rk, 128:256]
-        qi = lax.broadcasted_iota(jnp.int32, (rows, span), 0)
-        ei = lax.broadcasted_iota(jnp.int32, (rows, span), 1)
-        visible = (ei > qi) & (ei <= qi + WINDOW_LENGTH)
         for h in range(2):
             sc = lax.dot_general(qb[h, r, :], keys, (((1,), (1,)), ((), ())), preferred_element_type=f32)
             sc = jnp.where(visible, sc, -jnp.inf)
@@ -241,71 +269,88 @@
             ab[m, r, h * 128:(h + 1) * 128] = (o / tot).astype(bf16)
         for d in range(1, 4):
             a_copy(b, d).start()
-        return carry
-
-    lax.fori_loop(0, NZ, attend, 0)
-
-    for zs in range(4):
-        other = ((z + 4 - zs) % 4) // 2 != y
-        when(other, remote(ob.at[zs], ob.at[zs], oy_send.at[zs], oy_recv.at[zs], ypeer).wait_recv)
-
-    def a_wait(b, carry):
+
+    def a_wait(b):
         r = pl.ds(pl.multiple_of(b * rows, rows), rows)
         for d in range(1, 4):
             mm = (m + d) % 4
             remote(ab.at[mm, r, :], ab.at[mm, r, :], a_send.at[b, d], a_recv.at[b, mm], ypeer).wait_recv()
             a_copy(b, d).wait_send()
-        return carry
-
-    lax.fori_loop(0, NZ, a_wait, 0)
-
-    def partial(b):
-        r = pl.ds(pl.multiple_of(b * rows, rows), rows)
+
+    def partial(b, first, count):
+        r = pl.ds(pl.multiple_of(b * rows + first, count), count)
         acc = jnp.dot(ab[0, r, :], ob[0], preferred_element_type=f32)
         for mm in range(1, NM):
             acc += jnp.dot(ab[mm, r, :], ob[mm], preferred_element_type=f32)
         return acc
 
-    def r_copy(side, d, zd):
-        return remote(sb.at[d], rb.at[side, d], r_send.at[d], r_recv.at[side, d], at_z(zd))
-
-    def hop(side, d, inner):
-        def go():
-            sb[d] = partial(d).astype(bf16)
-
-            def add():
-                r_copy(side, d, z).wait_recv()
-                sb[d] = (partial(d) + rb[side, d].astype(f32)).astype(bf16)
-            pl.when(inner)(add)
-            r_copy(side, d, (z + 1) % 4 if side == 0 else (z + 3) % 4).start()
-        return go
-
-    for i in range(3):
-        dr, dl = 3 - i, i
-        pl.when(z < dr)(hop(0, dr, z > 0))
-        pl.when(z > dl)(hop(1, dl, z < 3))
-
-    out_acc = xb.shape and partial(z)
-    ss_acc = out_acc
-    zero = jnp.zeros_like(out_acc)
-
-    @pl.when(z > 0)
-    def _():
-        r_copy(0, z, (z + 1) % 4).wait_recv()
-
-    @pl.when(z == 0)
-    def _():
-        rb[0, z] = zero.astype(bf16)
-
-    @pl.when(z < 3)
-    def _():
-        r_copy(1, z, (z + 1) % 4).wait_recv()
-
-    @pl.when(z == 3)
-    def _():
-        rb[1, z] = zero.astype(bf16)
-
-    mixed = ss_acc + rb[0, z].astype(f32) + rb[1, z].astype(f32)
+    half = rows // 2
+
+    def r_copy(side, b, hf, zd):
+        r = pl.ds(hf * half, half)
+        return remote(sb.at[b, r, :], rb.at[side, b, r, :], r_send.at[b, hf], r_recv.at[side, b, hf], at_z(zd))
+
+    def hop(b):
+        right = b > z
+        side = jnp.where(right, 0, 1)
+        target = jnp.where(right, (z + 1) % 4, (z + 3) % 4)
+        inner = (right & (z > 0)) | (jnp.logical_not(right) & (z < 3))
+        for hf in range(2):
+            r = pl.ds(hf * half, half)
+            pacc[r, :] = partial(b, hf * half, half)
+
+            @pl.when(inner)
+            def _():
+                r_copy(side, b, hf, target).wait_recv()
+                sb[b, r, :] = (pacc[r, :] + rb[side, b, r, :].astype(f32)).astype(bf16)
+
+            @pl.when(jnp.logical_not(inner))
+            def _():
+                sb[b, r, :] = pacc[r, :].astype(bf16)
+
+            r_copy(side, b, hf, target).start()
+
+    def pick(a0, a1, a2, a3):
+        return jnp.where(z == 0, a0, jnp.where(z == 1, a1, jnp.where(z == 2, a2, a3)))
+
+    order = [pick(3, 3, 0, 0), pick(2, 0, 3, 1), pick(1, 2, 1, 2), z]
+    edge = (z == 0) | (z == 3)
+
+    def first_hop():
+        a_wait(order[0])
+        hop(order[0])
+
+    attend(order[0])
+    for h in range(2):
+        o_in = ob.at[2 * (1 - y) + h]
+        remote(o_in, o_in, oy_send.at[h], oy_recv.at[h], ypeer).wait_recv()
+        own_o[h][1].wait()
+    pl.when(edge)(first_hop)
+    attend(order[1])
+    pl.when(jnp.logical_not(edge))(first_hop)
+    attend(order[2])
+    a_wait(order[1])
+    hop(order[1])
+    attend(order[3])
+    a_wait(order[2])
+    hop(order[2])
+    a_wait(order[3])
+
+    pacc[...] = partial(z, 0, rows)
+    for hf in range(2):
+        r = pl.ds(hf * half, half)
+
+        @pl.when(z > 0)
+        def _():
+            r_copy(0, z, hf, z).wait_recv()
+            pacc[r, :] += rb[0, z, r, :].astype(f32)
+
+        @pl.when(z < 3)
+        def _():
+            r_copy(1, z, hf, z).wait_recv()
+            pacc[r, :] += rb[1, z, r, :].astype(f32)
+
+    mixed = pacc[...]
     ss[m] = jnp.broadcast_to(jnp.sum(mixed * mixed, axis=-1, keepdims=True), (rows, 128))
 
     def s_copy(d):
@@ -323,7 +368,8 @@
     for d in range(1, 4):
         s_copy(d).wait_send()
     for d in range(4):
-        when(z != d, r_copy(0, d, (z + 1) % 4).wait_send)
+        for hf in range(2):
+            when(z != d, r_copy(0, d, hf, (z + 1) % 4).wait_send)
     for cond, cp in pending:
         when(cond, cp.wait_send)
 
@@ -353,6 +399,8 @@
         out_specs=vmem,
         scratch_shapes=[
             pltpu.VMEM((4, 4, rows, cols), bf16),
+            pltpu.VMEM((4, 4, rows, cols), bf16),
+            pltpu.VMEM((4, depth, 512), bf16),
             pltpu.VMEM((4, 2 * depth, 512), bf16),
             pltpu.VMEM((4, 256, cols), bf16),
             pltpu.VMEM((3072, 256), bf16),
@@ -361,12 +409,13 @@
             pltpu.VMEM((2, 4, rows, cols), bf16),
             pltpu.VMEM((4, rows, cols), bf16),
             pltpu.VMEM((4, rows, 128), f32),
-            dma((7,)), dma((2, 4)), dma((4,)), dma((4,)), dma((4,)), dma((2, 4)), dma((2, 4)),
-            dma((4, 3)), dma((4, 3)), dma((4,)), dma((4,)), dma((2,)), dma((4,)), dma((4,)), dma((4,)),
-            dma((4,)), dma((4,)), dma((4, 4)), dma((4, 4)), dma((4,)), dma((2, 4)), dma((4,)), dma((4,)),
+            pltpu.VMEM((rows, cols), f32),
+            dma((9,)), dma((2, 4)), dma((4,)), dma((4,)), dma((4,)), dma((2, 4)), dma((2, 4)),
+            dma((4, 3)), dma((4, 3)), dma((4,)), dma((4,)), dma((4,)), dma((4,)), dma((4, 2)), dma((2,)), dma((2,)), dma((2,)),
+            dma((4,)), dma((4,)), dma((4, 4)), dma((4, 4)), dma((4, 2)), dma((2, 4, 2)), dma((4,)), dma((4,)),
         ],
         compiler_params=pltpu.CompilerParams(
-            collective_id=0, has_side_effects=True, vmem_limit_bytes=56 * 1024 * 1024,
+            collective_id=0, has_side_effects=True, vmem_limit_bytes=60 * 1024 * 1024,
         ),
     )(
         hidden_in, gain_in.reshape(4, 1, cols), w_query, key_weight, value_weight,

time: 336 us -> 228 us (0.68)
  Pallas kernels: 326 us -> 217 us
    pallas_call x1, Pallas kernels: 326 us -> 217 us  [fused(): pl.pallas_call(layer_kernel, name='layer', out_shape=jax.ShapeDtypeStruct...]
where the time goes in v2:
time: 228 us; the launch traced here: 227 us
  Pallas kernels  217 us (95%)
  local copies, waits for them, and re-layouts  6.33 us (3%)
  other arithmetic  3.3 us (1%)
    pallas_call x1, Pallas kernels, fused(): pl.pallas_call(layer_kernel, name='layer', out_shape=jax.ShapeDtypeStruct...  217 us

profile of v2, /device:TPU:19, one launch (start us, length us, event | category | flops | bytes accessed | tf_op | source)
XLA Modules:
  0.0 227.3 jit_solution(9773431601920182906)
XLA Ops:
  0.7 0.1 convert_bitcast_fusion
  0.8 1.9 fusion
  2.7 0.0 copy-start
  2.7 1.3 pad_maximum_fusion
  4.0 0.1 copy-done
  4.1 0.0 copy-start.1
  4.1 1.5 copy.14.wo
  5.7 0.0 copy-done.1
  5.7 0.0 copy-start.2
  5.7 0.0 copy-start.3
  5.7 1.1 copy.13.hidden
  6.8 0.0 copy-done.2
  6.8 0.7 reshape.45.gain_in
  7.5 0.0 copy-done.3
  7.5 0.6 reshape.48.gain_post
  8.1 217.0 %layer.1 = bf16[256,1344]{1,0:T(8,128)(2,1)} custom-call(bf16[256,1344]{1,0:T(8,128)(2,1)} %copy.13.hidden, f32[4,1,1344]{2,1,0:T(1,128)} %reshape.45.gain_in, bf16[672,1024]{1,0:T(8,128)(2,1)} %wq.1, bf16[672,512]{1,0:T(8,128)(2,1)} %wk.1, bf16[672,512]{1,0:T(8,128)(2,1)} %wv.1, f32[1,128]{1,0:T(1,128)} %bitcast.8, f32[1,128]{1,0:T(1,128)} %bitcast.9, ...), custom_call_target="tpu_custom_call" | custom-call | tf_op jit(solution)/shard_map/layer/pallas_call | solution.py:394
  225.1 2.2 copy.15
  (3 shorter events, 0.0 us)
Async XLA Ops:
  2.7 1.5 copy-start
  4.1 1.5 copy-start.1
  5.7 1.1 copy-start.2
  5.7 1.8 copy-start.3
